TPU v7x, 256 devices: a whole 4x4x8 slice. The times are simulated.
256 devices in a mesh: wide: 16 (over z, core), ctx: 16 (over y, x).
Axes of the slice: x: 4, y: 4, z: 8, core: 2. Of those that a mesh axis runs over, the one named last changes fastest.
Arguments:
- residual: float32 [256, 4096], P('wide', 'ctx'), may hold values from -40 to 40
- grad_out: float32 [256, 4096], P('wide', 'ctx'), may hold values from -6 to 6
- norm_gain: float32 [4096], P('ctx'), may hold values from 0.5 to 1.5
- w_gate: float32 [4096, 14336], P('ctx', 'wide'), may hold values from -0.09375 to 0.09375
- w_up: float32 [4096, 14336], P('ctx', 'wide'), may hold values from -0.09375 to 0.09375
- w_down: float32 [14336, 4096], P('wide', 'ctx'), may hold values from -0.046875 to 0.046875
- w_out: float32 [4096, 4096], P('wide', 'ctx'), may hold values from -0.09375 to 0.09375
- queries: float32 [256, 4096], P('ctx', 'wide'), may hold values from -12 to 12
- attn_out: float32 [256, 4096], P('ctx', 'wide'), may hold values from -3 to 3
- log_sum_exp: float32 [32, 256], P('wide', 'ctx')
- key_cache: float32 [16, 16384, 128], P('wide', 'ctx'), may hold values from -16 to 16
- value_cache: float32 [16, 16384, 128], P('wide', 'ctx'), may hold values from -6 to 6
Outputs:
- grad_w_gate: float32 [4096, 14336], P('ctx', 'wide')
- grad_w_up: float32 [4096, 14336], P('ctx', 'wide')
- grad_w_down: float32 [14336, 4096], P('wide', 'ctx')
- grad_w_out: float32 [4096, 4096], P('wide', 'ctx')
- grad_resid: float32 [256, 4096], P('wide', 'ctx')
- grad_queries: float32 [256, 4096], P('ctx', 'wide')
All inputs are finite; a program needn't handle non-finite values.
Results may differ from a plain program's by a relative error of at most 0.0003.
Values sent between devices are 32-bit elements; how exact they have to be, the bound alone decides.
A program may use at most 64 MiB of HBM per device.

v0:
```python
import functools
import math
import jax
import jax.numpy as jnp
from jax import lax
from jax.sharding import Mesh
from jax.sharding import PartitionSpec as P

KVH = 8
HD = 128
CTX = ("ctx_0", "ctx_1")
epsilon = 1e-05
highest = lax.Precision.HIGHEST


def swapped(block, axis, bit):
    count = lax.axis_size(axis)
    route = []
    for low in range(count):
        high = low | 1 << bit
        if high != low and high < count:
            route += [(low, high), (high, low)]
    return lax.ppermute(block, axis, route)


def side_by_side(arrays, axis, dim, along):
    ends, at = ([], 0)
    for a in arrays[:-1]:
        at += a.shape[along]
        ends.append(at)
    both = jnp.concatenate(arrays, axis=along)
    return tuple(jnp.split(lax.all_gather(both, axis, axis=dim, tiled=True), ends, axis=along))


def in_blocks(x, dim, length):
    shape = x.shape
    pieces = x.reshape(*shape[:dim], length, shape[dim] // length, *shape[dim + 1 :])
    return jnp.moveaxis(pieces, dim, 0)


def summed_on_arrival(x, axis, dim):
    pieces = in_blocks(x, dim, lax.axis_size(axis))
    arrived = lax.all_to_all(pieces, axis, split_axis=0, concat_axis=0, tiled=True)
    return arrived.sum(axis=0)


def one_axis_at_a_time(x, axes):
    return functools.reduce(lax.psum, axes, x)


def joined_along(pieces, dim):
    pieces = jnp.moveaxis(pieces, 0, dim)
    shape = pieces.shape
    return pieces.reshape(*shape[:dim], shape[dim] * shape[dim + 1], *shape[dim + 2 :])


def copy_for_each(x, axis):
    length = lax.axis_size(axis)
    return lax.all_to_all(jnp.broadcast_to(x[None], (length, *x.shape)), axis, 0, 0, tiled=True)


def collect(x, axis, dim):
    return joined_along(copy_for_each(x, axis), dim)


def rows_first(arrays, axis, dims):
    turned = [jnp.moveaxis(a, dim, 0) for a, dim in zip(arrays, dims)]
    widths = [t[0].size for t in turned]
    both = jnp.concatenate([t.reshape(-1, w) for t, w in zip(turned, widths)], axis=1)
    filled = lax.all_gather(both, axis, axis=0, tiled=True)
    pieces = jnp.split(filled, [sum(widths[:k]) for k in range(1, len(widths))], axis=1)
    return tuple(
        (
            jnp.moveaxis(b.reshape(-1, *t.shape[1:]), 0, dim)
            for b, t, dim in zip(pieces, turned, dims)
        )
    )


def matmul(left, right):
    return jnp.dot(left, right, precision=highest, preferred_element_type=jnp.float32)


def matmul_tn(left, right):
    return lax.dot_general(
        left, right, (((0,), (0,)), ((), ())), precision=highest, preferred_element_type=jnp.float32
    )


def matmul_nt(left, right):
    return lax.dot_general(
        left, right, (((1,), (1,)), ((), ())), precision=highest, preferred_element_type=jnp.float32
    )


def join_group(own_part, far_part, upper):
    joined = []
    for own_item, far_item, join_dim in zip(own_part, far_part, (1, 1, 0, 0)):
        lower_first = jnp.concatenate((own_item, far_item), axis=join_dim)
        upper_first = jnp.concatenate((far_item, own_item), axis=join_dim)
        joined.append(jnp.where(upper, upper_first, lower_first))
    return tuple(joined)


def halve_group(partial_sums, member, split):
    for bit_index in reversed(range(split.bit_length() - 1)):
        half_width = partial_sums.shape[1] // 2
        upper = member // (1 << bit_index) % 2 == 1
        lower_half = partial_sums[:, :half_width]
        upper_half = partial_sums[:, half_width:]
        kept_half = jnp.where(upper, upper_half, lower_half)
        sent_half = jnp.where(upper, lower_half, upper_half)
        partial_sums = kept_half + swapped(sent_half, "wide", bit_index)
    return partial_sums


def shards(
    residual,
    grad_out,
    norm_gain,
    w_gate,
    w_up,
    w_down,
    w_out,
    queries,
    attn_out,
    log_sum_exp,
    key_cache,
    value_cache,
):
    width = residual.shape[1] * lax.axis_size(CTX)
    all_resid, all_grad = side_by_side((residual, grad_out), "wide", 0, 1)
    gained = all_resid * norm_gain[None, :]
    gate_raw, up_raw, d_hidden, squares = lax.psum(
        (
            matmul(gained, w_gate),
            matmul(gained, w_up),
            matmul_nt(all_grad, w_down),
            jnp.sum(all_resid * all_resid, axis=1),
        ),
        CTX,
    )
    inv_rms = lax.rsqrt(squares / width + epsilon)
    normed = gained * inv_rms[:, None]
    gate_out = gate_raw * inv_rms[:, None]
    up_out = up_raw * inv_rms[:, None]
    sigmoid_gate = jax.nn.sigmoid(gate_out)
    activated = gate_out * sigmoid_gate
    hidden = activated * up_out
    grad_w_down = matmul_tn(hidden, all_grad)
    d_up = d_hidden * activated
    d_gate = d_hidden * up_out * sigmoid_gate * (1.0 + gate_out * (1.0 - sigmoid_gate))
    grad_w_gate = matmul_tn(normed, d_gate)
    grad_w_up = matmul_tn(normed, d_up)
    own_rows = residual.shape[0]
    d_normed = summed_on_arrival(matmul_nt(d_gate, w_gate) + matmul_nt(d_up, w_up), "wide", 0)
    scaled = d_normed * norm_gain[None, :]
    row_dot = one_axis_at_a_time(jnp.sum(residual * scaled, axis=1), CTX)
    own_inv = lax.dynamic_slice_in_dim(inv_rms, lax.axis_index("wide") * own_rows, own_rows, 0)
    cubed = own_inv * own_inv * own_inv
    grad_resid = (
        grad_out + own_inv[:, None] * scaled - residual * (cubed * row_dot / width)[:, None]
    )
    gathered_resid = collect(grad_resid, "wide", 0)
    d_attn = summed_on_arrival(matmul_nt(gathered_resid, w_out), CTX, 0)
    all_queries, all_outputs, all_dattn, all_lse = rows_first(
        (queries, attn_out, d_attn, log_sum_exp), CTX, (0, 0, 0, 1)
    )
    grad_w_out = matmul_tn(all_outputs, gathered_resid)
    rows_total = all_queries.shape[0]
    head_dim = HD
    local_heads = all_queries.shape[1] // head_dim
    delta = jnp.sum((all_dattn * all_outputs).reshape(rows_total, local_heads, head_dim), axis=2).T
    split = lax.axis_size("wide") // KVH
    member = lax.axis_index("wide") % split
    group = (all_queries, all_dattn, all_lse, delta)
    partner = swapped(group, "wide", 0)
    upper = member // (1 << 0) % 2 == 1
    group = join_group(group, partner, upper)
    group_queries, group_dattn, group_lse, group_delta = group
    group_count = group_queries.shape[1] // head_dim
    query_rows = (
        group_queries.reshape(rows_total, group_count, head_dim)
        .transpose(1, 0, 2)
        .reshape(group_count * rows_total, head_dim)
    )
    dout_rows = (
        group_dattn.reshape(rows_total, group_count, head_dim)
        .transpose(1, 0, 2)
        .reshape(group_count * rows_total, head_dim)
    )
    lse_rows = group_lse.reshape(group_count * rows_total)
    delta_rows = group_delta.reshape(group_count * rows_total)
    keys_local = key_cache[0]
    values_local = value_cache[0]
    key_count = keys_local.shape[0]
    ctx_count = lax.axis_size(CTX)
    context = key_count * ctx_count * split
    key_base = member * (key_count * ctx_count) + lax.axis_index(CTX) * key_count
    query_pos = jnp.tile(jnp.arange(rows_total, dtype=jnp.int32), group_count) + (
        context - rows_total
    )
    scale = 1.0 / math.sqrt(head_dim)
    block = min(512, key_count)
    accum = jnp.zeros((group_count * rows_total, head_dim), jnp.float32)
    for block_index in range(key_count // block):
        key_block = keys_local[block_index * block : (block_index + 1) * block]
        value_block = values_local[block_index * block : (block_index + 1) * block]
        key_pos = key_base + block_index * block + jnp.arange(block, dtype=jnp.int32)
        scores = matmul_nt(query_rows, key_block) * scale
        probs = jnp.where(
            key_pos[None, :] <= query_pos[:, None], jnp.exp(scores - lse_rows[:, None]), 0.0
        )
        dprobs = matmul_nt(dout_rows, value_block)
        accum = accum + matmul(probs * (dprobs - delta_rows[:, None]), key_block)
    dq_group = (
        (accum * scale)
        .reshape(group_count, rows_total, head_dim)
        .transpose(1, 0, 2)
        .reshape(rows_total, group_count * head_dim)
    )
    halved = halve_group(dq_group, member, split)
    grad_queries = summed_on_arrival(halved, CTX, 0)
    return (grad_w_gate, grad_w_up, grad_w_down, grad_w_out, grad_resid, grad_queries)


def solution(mesh):
    torus = Mesh(mesh.devices.reshape(mesh.shape["wide"], 4, 4), ("wide", "ctx_0", "ctx_1"))
    return jax.shard_map(
        shards,
        mesh=torus,
        in_specs=(
            P("wide", CTX),
            P("wide", CTX),
            P(CTX),
            P(CTX, "wide"),
            P(CTX, "wide"),
            P("wide", CTX),
            P("wide", CTX),
            P(CTX, "wide"),
            P(CTX, "wide"),
            P("wide", CTX),
            P("wide", CTX, None),
            P("wide", CTX, None),
        ),
        out_specs=(
            P(CTX, "wide"),
            P(CTX, "wide"),
            P("wide", CTX),
            P("wide", CTX),
            P("wide", CTX),
            P(CTX, "wide"),
        ),
        check_vma=False,
    )
```

profile of v0, /device:TPU:1, one launch (start us, length us, event | category | flops | bytes accessed | tf_op | source)
XLA Modules:
  0.0 293.4 jit_solution(3167440317429720697)
XLA Ops:
  8.0 22.7 %all_gather.6 = f32[256,512]{1,0:T(8,128)S(1)} all-gather(f32[16,512]{1,0:T(8,128)S(1)} %pad_maximum_fusion.1), channel_id=1, replica_groups=mesh['wide'=16,'ctx_0'=4,'ctx_1'=4] {'wide'}, dimensions={0}, use_global_device_ids=true | all-gather | bytes 557056 | tf_op jit(solution)/shard_map/all_gather | solution.py:32
  30.8 3.2 %fusion.59 = f32[256,896]{1,0:T(8,128)} fusion(f32[896,256]{1,0:T(8,128)} %param.17, f32[256,512]{1,0:T(8,128)S(1)} %all_gather.6), kind=kOutput, calls=%fused_computation.64 | convolution fusion | flops 704643072 | bytes 2097152 | tf_op jit(solution)/shard_map/dot_general | solution.py:91
  34.0 2.0 fusion.68
  35.9 2.0 fusion.69
  38.0 33.9 %psum.42 = f32[256]{0:T(256)S(1)} all-reduce(f32[256]{0:T(256)S(1)} %multiply_reduce_fusion), channel_id=1, replica_groups=mesh['wide'=16,'ctx_0'=4,'ctx_1'=4] {'ctx_0','ctx_1'}, use_global_device_ids=true, to_apply=%region_1.0 | all-reduce | flops 256 | bytes 2048 | tf_op jit(solution)/shard_map/psum | solution.py:134
  71.9 67.0 %all-reduce.3.cloned.1.call-done = (f32[256,896]{1,0:T(8,128)}, f32[256,896]{1,0:T(8,128)}, f32[256,896]{1,0:T(8,128)}) async-done(((f32[256,896]{1,0:T(8,128)}, f32[256,896]{1,0:T(8,128)}, f32[256,896]{1,0:T(8,128)}), (f32[256,896]{1,0:T(8,128)}, f32[256,896]{1,0:T(8,128)}, f32[256,896]{1,0:T(8,128)})) %all-reduce.3.cloned.1.call-update) | async-done | bytes 2752528 | tf_op jit(solution)/shard_map/psum | solution.py:134
  138.9 2.3 add_multiply_fusion
  142.3 1.9 convolution_add_fusion
  144.2 8.7 %all-to-all-start = ((f32[16,16,256]{2,1,0:T(8,128)}), f32[16,16,256]{2,1,0:T(8,128)S(1)}, u32[]{:S(2)}, u32[]{:S(2)}) async-start(f32[16,16,256]{2,1,0:T(8,128)} %bitcast), calls=%async_computation | async-start | bytes 524288 | tf_op jit(solution)/shard_map/all_to_all | solution.py:43
  152.9 11.6 %all-to-all-done = f32[16,16,256]{2,1,0:T(8,128)S(1)} async-done(((f32[16,16,256]{2,1,0:T(8,128)}), f32[16,16,256]{2,1,0:T(8,128)S(1)}, u32[]{:S(2)}, u32[]{:S(2)}) %all-to-all-start) | async-done | bytes 262176 | tf_op jit(solution)/shard_map/all_to_all | solution.py:43
  164.7 7.7 %psum.46 = f32[16]{0:T(128)S(1)} all-reduce(f32[16]{0:T(128)S(1)} %multiply_reduce_fusion.1), channel_id=1, replica_groups=mesh['wide'=16,'ctx_0'=4,'ctx_1'=4] {'ctx_0'}, use_global_device_ids=true, to_apply=%region_7.0 | all-reduce | flops 16 | bytes 128 | tf_op jit(solution)/shard_map/psum | solution.py:48
  172.4 7.4 %psum.47 = f32[16]{0:T(128)S(1)} all-reduce(f32[16]{0:T(128)S(1)} %psum.46), channel_id=1, replica_groups=mesh['wide'=16,'ctx_0'=4,'ctx_1'=4] {'ctx_1'}, use_global_device_ids=true, to_apply=%region_8.0 | all-reduce | flops 16 | bytes 128 | tf_op jit(solution)/shard_map/psum | solution.py:48
  180.0 18.1 %all_to_all.20 = f32[16,16,256]{2,1,0:T(8,128)S(1)} all-to-all(f32[16,16,256]{2,1,0:T(8,128)S(1)} %broadcast_in_dim.6), channel_id=1, replica_groups=mesh['wide'=16,'ctx_0'=4,'ctx_1'=4] {'wide'}, dimensions={0} | all-to-all | bytes 524288 | tf_op jit(solution)/shard_map/all_to_all | solution.py:59
  199.9 3.5 %all-to-all-start.2 = ((f32[16,16,256]{2,1,0:T(8,128)}), f32[16,16,256]{2,1,0:T(8,128)S(1)}, u32[]{:S(2)}, u32[]{:S(2)}) async-start(f32[16,16,256]{2,1,0:T(8,128)} %fusion.54), calls=%async_computation.2 | async-start | bytes 524288 | tf_op jit(solution)/shard_map/all_to_all | solution.py:43
  205.3 7.2 %all-to-all-done.2 = f32[16,16,256]{2,1,0:T(8,128)S(1)} async-done(((f32[16,16,256]{2,1,0:T(8,128)}), f32[16,16,256]{2,1,0:T(8,128)S(1)}, u32[]{:S(2)}, u32[]{:S(2)}) %all-to-all-start.2) | async-done | bytes 262176 | tf_op jit(solution)/shard_map/all_to_all | solution.py:43
  212.6 17.2 %all_gather.7 = f32[256,770]{1,0:T(8,128)S(1)} all-gather(f32[16,770]{1,0:T(8,128)S(1)} %pad_maximum_fusion), channel_id=1, replica_groups=mesh['wide'=16,'ctx_0'=4,'ctx_1'=4] {'ctx_0','ctx_1'}, dimensions={0}, use_global_device_ids=true | all-gather | bytes 837760 | tf_op jit(solution)/shard_map/all_gather | solution.py:70
  230.0 5.9 %collective-permute-start.2 = (f32[256,256]{0,1:T(8,128)S(1)}, f32[256,256]{0,1:T(8,128)}, u32[]{:S(2)}, u32[]{:S(2)}) collective-permute-start(f32[256,256]{0,1:T(8,128)S(1)} %copy.53), channel_id=1, source_target_pairs={{0,16},{16,0},{32,48},{48,32},{64,80},{80,64},{96,112},{112,96},{1... | collective-permute-start | bytes 786440 | tf_op jit(solution)/shard_map/ppermute | solution.py:23
  236.7 3.7 %fusion.42 = f32[256,896]{1,0:T(8,128)} fusion(f32[256,896]{1,0:T(8,128)} %get-tuple-element.6, f32[256,512]{1,0:T(8,128)S(1)} %all_gather.6, f32[256]{0:T(256)} %copy-done.23, f32[256]{0:T(256)} %param.14, f32[256,896]{1,0:T(8,128)} %get-tuple-element.7), kind=kOutput, calls=%fused_computation.43 | convolution fusion | flops 706150400 | bytes 3017728 | tf_op jit(solution)/shard_map/dot_general | solution.py:85
  244.6 4.1 %fusion.44 = f32[1024,512]{1,0:T(8,128)} fusion(f32[1024,128]{1,0:T(8,128)S(1)} %bitcast.66, f32[1,1024,128]{2,1,0:T(8,128)} %param.23), kind=kOutput, calls=%fused_computation.45 | convolution fusion | flops 805306368 | bytes 2883584 | tf_op jit(solution)/shard_map/dot_general | solution.py:91
  248.6 2.8 fusion.49
  251.5 2.1 fusion.38
  253.6 2.0 copy.42
  255.6 3.0 %fusion.47 = f32[1024,512]{1,0:T(8,128)S(1)} fusion(f32[1024,128]{1,0:T(8,128)} %bitcast.68, f32[1,1024,128]{2,1,0:T(8,128)} %param.22), kind=kOutput, calls=%fused_computation.48 | convolution fusion | flops 805306368 | bytes 2883584 | tf_op jit(solution)/shard_map/dot_general | solution.py:91
  258.7 1.8 fusion.52
  260.5 2.2 fusion
  262.8 3.3 %fusion.19 = f32[1024,128]{1,0:T(8,128)} fusion(f32[1024,128]{1,0:T(8,128)S(1)} %fusion, f32[1024,512]{1,0:T(8,128)S(1)} %fusion.49, f32[1024,512]{1,0:T(8,128)S(1)} %fusion.52, f32[1024]{0:T(1024)S(1)} %bitcast.76, f32[1024]{0:T(1024)S(1)} %bitcast.78, s32[512]{0:T(512)S(1)} %copy-done.25, s32[1024]{0:T(1024)S(1)} %bitcast.74, ...), kind=kOutput, calls=%fused_computation.17 | convolution fusion | flops 808714240 | bytes 5519360 | tf_op jit(solution)/shard_map/dot_general | solution.py:81
  266.1 1.2 copy.49
  268.1 4.2 %fusion.34 = f32[896,256]{1,0:T(8,128)} fusion(f32[256,896]{1,0:T(8,128)} %get-tuple-element.8, f32[256]{0:T(256)S(1)} %copy-done.24, f32[256,512]{1,0:T(8,128)S(1)} %all_gather.6, f32[256,896]{1,0:T(8,128)} %get-tuple-element.7), kind=kOutput, calls=%fused_computation.31 | convolution fusion | flops 706248704 | bytes 3015680 | tf_op jit(solution)/shard_map/dot_general | solution.py:85
  273.2 4.3 %all-to-all-start.3 = ((f32[16,16,256]{2,1,0:T(8,128)}), f32[16,16,256]{2,1,0:T(8,128)S(1)}, u32[]{:S(2)}, u32[]{:S(2)}) async-start(f32[16,16,256]{2,1,0:T(8,128)} %bitcast.23), calls=%async_computation.3 | async-start | bytes 524288 | tf_op jit(solution)/shard_map/all_to_all | solution.py:43
  277.5 2.0 fusion.66
  279.5 2.2 fusion.84
  281.8 4.1 %all-to-all-done.3 = f32[16,16,256]{2,1,0:T(8,128)S(1)} async-done(((f32[16,16,256]{2,1,0:T(8,128)}), f32[16,16,256]{2,1,0:T(8,128)S(1)}, u32[]{:S(2)}, u32[]{:S(2)}) %all-to-all-start.3) | async-done | bytes 262176 | tf_op jit(solution)/shard_map/all_to_all | solution.py:43
  (101 shorter events, 13.5 us)
Async XLA Ops:
  7.2 26.8 %copy-start = (f32[256,896]{1,0:T(8,128)S(1)}, f32[256,896]{1,0:T(8,128)}, u32[]{:S(2)}) copy-start(f32[256,896]{1,0:T(8,128)} %param.15) | copy-start | bytes 2752516
  7.2 26.8 %copy-start.19 = (f32[256]{0:T(256)S(1)}, f32[256]{0:T(256)}, u32[]{:S(2)}) copy-start(f32[256]{0:T(256)} %param.14) | copy-start | bytes 3076
  7.2 131.7 %all-reduce.3.cloned.1.call-start = ((), (), s32[]{:S(2)}) async-start(), calls=%async_computation.4 | async-start | bytes 5505024 | tf_op jit(solution)/shard_map/psum | solution.py:134
  30.8 5.2 %copy-start.10 = (f32[256,896]{1,0:T(8,128)S(1)}, f32[256,896]{1,0:T(8,128)}, u32[]{:S(2)}) copy-start(f32[256,896]{1,0:T(8,128)} %param.16) | copy-start | bytes 2752516
  71.9 107.8 %copy-start.23 = (f32[256]{0:T(256)}, f32[256]{0:T(256)S(1)}, u32[]{:S(2)}) copy-start(f32[256]{0:T(256)S(1)} %add_rsqrt_fusion) | copy-start | bytes 3076
  138.9 3.4 %copy-start.11 = (f32[256,896]{1,0:T(8,128)S(1)}, f32[256,896]{1,0:T(8,128)}, u32[]{:S(2)}) copy-start(f32[256,896]{1,0:T(8,128)} %get-tuple-element.7) | copy-start | bytes 2752516
  138.9 3.4 %copy-start.12 = (f32[256,896]{1,0:T(8,128)S(1)}, f32[256,896]{1,0:T(8,128)}, u32[]{:S(2)}) copy-start(f32[256,896]{1,0:T(8,128)} %get-tuple-element.6) | copy-start | bytes 2752516
  141.2 3.0 %copy-start.2 = (f32[256,896]{1,0:T(8,128)}, f32[256,896]{1,0:T(8,128)S(1)}, u32[]{:S(2)}) copy-start(f32[256,896]{1,0:T(8,128)S(1)} %add_multiply_fusion) | copy-start | bytes 2752516
  142.3 22.3 %copy-start.15 = (f32[16,256]{1,0:T(8,128)S(1)}, f32[16,256]{1,0:T(8,128)}, u32[]{:S(2)}) copy-start(f32[16,256]{1,0:T(8,128)} %param.12) | copy-start | bytes 49156
  142.3 37.6 %copy-start.17 = (f32[16,256]{1,0:T(8,128)S(1)}, f32[16,256]{1,0:T(8,128)}, u32[]{:S(2)}) copy-start(f32[16,256]{1,0:T(8,128)} %param.13) | copy-start | bytes 49156
  142.3 56.5 %copy-start.14 = (f32[256,256]{1,0:T(8,128)S(1)}, f32[256,256]{1,0:T(8,128)}, u32[]{:S(2)}) copy-start(f32[256,256]{1,0:T(8,128)} %param.18) | copy-start | bytes 786436
  144.2 59.2 %copy-start.27 = (f32[2,16]{1,0:T(2,128)S(1)}, f32[2,16]{1,0:T(2,128)}, u32[]{:S(2)}) copy-start(f32[2,16]{1,0:T(2,128)} %param.21) | copy-start | bytes 388
  144.2 68.3 %copy-start.21 = (f32[16,256]{1,0:T(8,128)S(1)}, f32[16,256]{1,0:T(8,128)}, u32[]{:S(2)}) copy-start(f32[16,256]{1,0:T(8,128)} %param.20) | copy-start | bytes 49156
  144.2 68.3 %copy-start.22 = (f32[16,256]{1,0:T(8,128)S(1)}, f32[16,256]{1,0:T(8,128)}, u32[]{:S(2)}) copy-start(f32[16,256]{1,0:T(8,128)} %param.19) | copy-start | bytes 49156
  144.2 20.3 %all-to-all-start = ((f32[16,16,256]{2,1,0:T(8,128)}), f32[16,16,256]{2,1,0:T(8,128)S(1)}, u32[]{:S(2)}, u32[]{:S(2)}) async-start(f32[16,16,256]{2,1,0:T(8,128)} %bitcast), calls=%async_computation | async-start | bytes 524288 | tf_op jit(solution)/shard_map/all_to_all | solution.py:43
  179.9 49.9 %copy-start.16 = (f32[16,256]{1,0:T(8,128)}, f32[16,256]{1,0:T(8,128)S(1)}, u32[]{:S(2)}) copy-start(f32[16,256]{1,0:T(8,128)S(1)} %multiply_subtract_fusion) | copy-start | bytes 49156
  199.9 12.6 %all-to-all-start.2 = ((f32[16,16,256]{2,1,0:T(8,128)}), f32[16,16,256]{2,1,0:T(8,128)S(1)}, u32[]{:S(2)}, u32[]{:S(2)}) async-start(f32[16,16,256]{2,1,0:T(8,128)} %fusion.54), calls=%async_computation.2 | async-start | bytes 524288 | tf_op jit(solution)/shard_map/all_to_all | solution.py:43
  229.7 10.7 %copy-start.4 = (f32[256,770]{1,0:T(8,128)}, f32[256,770]{1,0:T(8,128)S(1)}, u32[]{:S(2)}) copy-start(f32[256,770]{1,0:T(8,128)S(1)} %all_gather.7) | copy-start | bytes 2365444
  230.0 12.5 %collective-permute-start.2 = (f32[256,256]{0,1:T(8,128)S(1)}, f32[256,256]{0,1:T(8,128)}, u32[]{:S(2)}, u32[]{:S(2)}) collective-permute-start(f32[256,256]{0,1:T(8,128)S(1)} %copy.53), channel_id=1, source_target_pairs={{0,16},{16,0},{32,48},{48,32},{64,80},{80,64},{96,112},{112,96},{1... | collective-permute-start | bytes 786440 | tf_op jit(solution)/shard_map/ppermute | solution.py:23
  235.9 5.5 %collective-permute-start.1 = (f32[2,256]{0,1:T(8,128)S(1)}, f32[2,256]{0,1:T(8,128)}, u32[]{:S(2)}, u32[]{:S(2)}) collective-permute-start(f32[2,256]{0,1:T(8,128)S(1)} %slice_bitcast_fusion), channel_id=1, source_target_pairs={{0,16},{16,0},{32,48},{48,32},{64,80},{80,64},{96,112},{112,96},{1... | collective-permute-start | bytes 6152 | tf_op jit(solution)/shard_map/ppermute | solution.py:23
  236.2 6.2 %collective-permute-start.3 = (f32[2,256]{1,0:T(2,128)S(1)}, f32[2,256]{1,0:T(2,128)S(1)}, u32[]{:S(2)}, u32[]{:S(2)}) collective-permute-start(f32[2,256]{1,0:T(2,128)S(1)} %bitcast.80), channel_id=1, source_target_pairs={{0,16},{16,0},{32,48},{48,32},{64,80},{80,64},{96,112},{112,96},{1... | collective-permute-start | bytes 6152 | tf_op jit(solution)/shard_map/ppermute | solution.py:23
  241.3 10.2 %collective-permute-start = (f32[256,256]{0,1:T(8,128)}, f32[256,256]{0,1:T(8,128)}, u32[]{:S(2)}, u32[]{:S(2)}) collective-permute-start(f32[256,256]{0,1:T(8,128)} %copy.52), channel_id=1, source_target_pairs={{0,16},{16,0},{32,48},{48,32},{64,80},{80,64},{96,112},{112,96},{1... | collective-permute-start | bytes 786440 | tf_op jit(solution)/shard_map/ppermute | solution.py:23
  243.8 4.9 %copy-start.13 = (f32[1,1024,128]{2,1,0:T(8,128)S(1)}, f32[1,1024,128]{2,1,0:T(8,128)}, u32[]{:S(2)}) copy-start(f32[1,1024,128]{2,1,0:T(8,128)} %param.23) | copy-start | bytes 1572868
  255.6 3.0 %copy-start.6 = (f32[4,256,128]{2,1,0:T(8,128)S(1)}, f32[4,256,128]{2,1,0:T(8,128)}, u32[]{:S(2)}) copy-start(f32[4,256,128]{2,1,0:T(8,128)} %copy.42) | copy-start | bytes 1572868
  255.6 3.0 %copy-start.9 = (f32[1,1024,128]{2,1,0:T(8,128)S(1)}, f32[1,1024,128]{2,1,0:T(8,128)}, u32[]{:S(2)}) copy-start(f32[1,1024,128]{2,1,0:T(8,128)} %param.22) | copy-start | bytes 1572868
  260.5 2.2 copy-start.25
  262.8 5.3 %copy-start.24 = (f32[256]{0:T(256)S(1)}, f32[256]{0:T(256)}, u32[]{:S(2)}) copy-start(f32[256]{0:T(256)} %copy-done.23) | copy-start | bytes 3076
  267.4 4.9 %collective-permute-start.4 = (f32[256,256]{0,1:T(8,128)S(1)}, f32[256,256]{0,1:T(8,128)S(1)}, u32[]{:S(2)}, u32[]{:S(2)}) collective-permute-start(f32[256,256]{0,1:T(8,128)S(1)} %slice_select_fusion), channel_id=1, source_target_pairs={{0,16},{16,0},{32,48},{48,32},{64,80},{80,64},{96,112},{112,96},{1... | collective-permute-start | bytes 786440 | tf_op jit(solution)/shard_map/ppermute | solution.py:23
  272.3 5.2 %copy-start.3 = (f32[256,896]{1,0:T(8,128)S(1)}, f32[256,896]{1,0:T(8,128)}, u32[]{:S(2)}) copy-start(f32[256,896]{1,0:T(8,128)} %copy-done.2) | copy-start | bytes 2752516
  272.3 5.2 %copy-start.20 = (f32[256]{0:T(256)S(1)}, f32[256]{0:T(256)}, u32[]{:S(2)}) copy-start(f32[256]{0:T(256)} %param.14) | copy-start | bytes 3076
  272.3 7.2 %copy-start.8 = (f32[16,16,256]{2,1,0:T(8,128)S(1)}, f32[16,16,256]{2,1,0:T(8,128)}, u32[]{:S(2)}) copy-start(f32[16,16,256]{2,1,0:T(8,128)} %copy-done.7) | copy-start | bytes 786436
  273.2 12.7 %all-to-all-start.3 = ((f32[16,16,256]{2,1,0:T(8,128)}), f32[16,16,256]{2,1,0:T(8,128)S(1)}, u32[]{:S(2)}, u32[]{:S(2)}) async-start(f32[16,16,256]{2,1,0:T(8,128)} %bitcast.23), calls=%async_computation.3 | async-start | bytes 524288 | tf_op jit(solution)/shard_map/all_to_all | solution.py:43
  (5 other events, 7.0 us)
Sparse Core Ops, SparseCore 0:
  38.0 100.8 all-reduce.2
where the time goes:
time: 294 us; the launch traced here: 293 us
  blocking collectives  107 us (36%)
  waiting for transfers between devices  89.9 us (31%)
  matrix products  40.7 us (14%)
  starting transfers between devices  23.9 us (8%)
  between operations  14.5 us (5%)
  local copies, waits for them, and re-layouts  8.82 us (3%)
  other arithmetic  8.64 us (3%)
    psum x1, waiting for transfers between devices, shards(): lax.psum((matmul(gained, w_gate), matmul(gained, w_up), matmul_nt(all_gra...  67 us
    psum x1, blocking collectives, shards(): lax.psum((matmul(gained, w_gate), matmul(gained, w_up), matmul_nt(all_gra...  33.9 us
    all_to_all x3, waiting for transfers between devices, summed_on_arrival(): lax.all_to_all(pieces, axis, split_axis=0, concat_axis=0, tiled=True)  22.9 us
    all_gather x1, blocking collectives, side_by_side(): lax.all_gather(both, axis, axis=dim, tiled=True)  22.7 us
    dot_general x8, matrix products, matmul_nt(): lax.dot_general(left, right, (((1,), (1,)), ((), ())), precision=highest,...  19 us
    all_to_all x1, blocking collectives, copy_for_each(): lax.all_to_all(jnp.broadcast_to(x[None], (length, *x.shape)), axis, 0, 0,...  18.1 us
    all_gather x1, blocking collectives, rows_first(): filled = lax.all_gather(both, axis, axis=0, tiled=True)  17.2 us
    all_to_all x3, starting transfers between devices, summed_on_arrival(): lax.all_to_all(pieces, axis, split_axis=0, concat_axis=0, tiled=True)  16.5 us
  transfers between devices with their start and end apart: 9, of which 4 were waited for; matrix products, arithmetic and copies ran while one was open for 8% of the time, Pallas kernels for 0%

commit v1 on v0

--- a/solution.py
+++ b/solution.py
@@ -132,13 +132,16 @@
     all_resid, all_grad = side_by_side((residual, grad_out), "wide", 0, 1)
     gained = all_resid * norm_gain[None, :]
     gate_raw, up_raw, d_hidden, squares = lax.psum(
-        (
-            matmul(gained, w_gate),
-            matmul(gained, w_up),
-            matmul_nt(all_grad, w_down),
-            jnp.sum(all_resid * all_resid, axis=1),
+        lax.psum(
+            (
+                matmul(gained, w_gate),
+                matmul(gained, w_up),
+                matmul_nt(all_grad, w_down),
+                jnp.sum(all_resid * all_resid, axis=1),
+            ),
+            "ctx_0",
         ),
-        CTX,
+        "ctx_1",
     )
     inv_rms = lax.rsqrt(squares / width + epsilon)
     normed = gained * inv_rms[:, None]

time: 294 us -> 342 us (1.16)
  waiting for transfers between devices: 89.9 us -> 157 us
  blocking collectives: 107 us -> 88.3 us
    psum x0 -> x1, waiting for transfers between devices: none -> 61.7 us  [shards(): lax.psum(lax.psum((matmul(gained, w_gate), matmul(gained, w_up), matmul_n...]
    psum x1, blocking collectives: 33.9 us -> 6.59 us  [shards(): lax.psum((matmul(gained, w_gate), matmul(gained, w_up), matmul_nt(all_gra...]
    psum x0 -> x1, blocking collectives: none -> 8.39 us  [shards(): lax.psum(lax.psum((matmul(gained, w_gate), matmul(gained, w_up), matmul_n...]
    psum x1, waiting for transfers between devices: 67 us -> 72.1 us  [shards(): lax.psum((matmul(gained, w_gate), matmul(gained, w_up), matmul_nt(all_gra...]
  transfers between devices with their start and end apart: 9 -> 10, of which waited for: 4 -> 5; matrix products, arithmetic and copies ran while one was open for 8% -> 7% of each run, Pallas kernels for 0% -> 0%
where the time goes in v1:
time: 342 us; the launch traced here: 341 us
  waiting for transfers between devices  157 us (46%)
  blocking collectives  88.3 us (26%)
  matrix products  40.7 us (12%)
  starting transfers between devices  23.3 us (7%)
  between operations  14.5 us (4%)
  local copies, waits for them, and re-layouts  8.83 us (3%)
  other arithmetic  8.64 us (3%)
    psum x1, waiting for transfers between devices, shards(): lax.psum((matmul(gained, w_gate), matmul(gained, w_up), matmul_nt(all_gra...  72.1 us
    psum x1, waiting for transfers between devices, shards(): lax.psum(lax.psum((matmul(gained, w_gate), matmul(gained, w_up), matmul_n...  61.7 us
    all_to_all x3, waiting for transfers between devices, summed_on_arrival(): lax.all_to_all(pieces, axis, split_axis=0, concat_axis=0, tiled=True)  22.9 us
    all_gather x1, blocking collectives, side_by_side(): lax.all_gather(both, axis, axis=dim, tiled=True)  22.7 us
    dot_general x8, matrix products, matmul_nt(): lax.dot_general(left, right, (((1,), (1,)), ((), ())), precision=highest,...  19 us
    all_to_all x1, blocking collectives, copy_for_each(): lax.all_to_all(jnp.broadcast_to(x[None], (length, *x.shape)), axis, 0, 0,...  18.4 us
    all_gather x1, blocking collectives, rows_first(): filled = lax.all_gather(both, axis, axis=0, tiled=True)  17.2 us
    all_to_all x3, starting transfers between devices, summed_on_arrival(): lax.all_to_all(pieces, axis, split_axis=0, concat_axis=0, tiled=True)  15.8 us
  transfers between devices with their start and end apart: 10, of which 5 were waited for; matrix products, arithmetic and copies ran while one was open for 7% of the time, Pallas kernels for 0%

profile of v1, /device:TPU:1, one launch (start us, length us, event | category | flops | bytes accessed | tf_op | source)
XLA Modules:
  0.0 340.9 jit_solution(17418590298736817401)
XLA Ops:
  8.0 22.7 %all_gather.6 = f32[256,512]{1,0:T(8,128)S(1)} all-gather(f32[16,512]{1,0:T(8,128)S(1)} %pad_maximum_fusion.1), channel_id=1, replica_groups=mesh['wide'=16,'ctx_0'=4,'ctx_1'=4] {'wide'}, dimensions={0}, use_global_device_ids=true | all-gather | bytes 557056 | tf_op jit(solution)/shard_map/all_gather | solution.py:32
  30.8 3.2 fusion.59
  34.0 2.0 fusion.68
  35.9 2.0 fusion.69
  38.0 72.1 %all-reduce.7.cloned.1.call-done = (f32[256,896]{1,0:T(8,128)}, f32[256,896]{1,0:T(8,128)}, f32[256,896]{1,0:T(8,128)}) async-done(((f32[256,896]{1,0:T(8,128)}, f32[256,896]{1,0:T(8,128)}, f32[256,896]{1,0:T(8,128)}), (f32[256,896]{1,0:T(8,128)}, f32[256,896]{1,0:T(8,128)}, f32[256,896]{1,0:T(8,128)})) %all-reduce.7.cloned.1.call-update) | async-done | bytes 2752528 | tf_op jit(solution)/shard_map/psum | solution.py:135
  110.2 6.6 %psum.70 = f32[256]{0:T(256)S(1)} all-reduce(f32[256]{0:T(256)S(1)} %multiply_reduce_fusion), channel_id=1, replica_groups=mesh['wide'=16,'ctx_0'=4,'ctx_1'=4] {'ctx_0'}, use_global_device_ids=true, to_apply=%region_1.0 | all-reduce | flops 256 | bytes 2048 | tf_op jit(solution)/shard_map/psum | solution.py:135
  116.8 8.4 %psum.71 = f32[256]{0:T(256)S(1)} all-reduce(f32[256]{0:T(256)S(1)} %psum.70), channel_id=1, replica_groups=mesh['wide'=16,'ctx_0'=4,'ctx_1'=4] {'ctx_1'}, use_global_device_ids=true, to_apply=%region_2.0 | all-reduce | flops 256 | bytes 2048 | tf_op jit(solution)/shard_map/psum | solution.py:134
  125.2 61.7 %all-reduce.5.cloned.1.call-done = (f32[256,896]{1,0:T(8,128)}, f32[256,896]{1,0:T(8,128)}, f32[256,896]{1,0:T(8,128)}) async-done(((f32[256,896]{1,0:T(8,128)}, f32[256,896]{1,0:T(8,128)}, f32[256,896]{1,0:T(8,128)}), (f32[256,896]{1,0:T(8,128)}, f32[256,896]{1,0:T(8,128)}, f32[256,896]{1,0:T(8,128)})) %all-reduce.5.cloned.1.call-update) | async-done | bytes 2752528 | tf_op jit(solution)/shard_map/psum | solution.py:134
  186.9 2.3 add_multiply_fusion
  190.3 1.9 convolution_add_fusion
  192.3 8.0 %all-to-all-start = ((f32[16,16,256]{2,1,0:T(8,128)}), f32[16,16,256]{2,1,0:T(8,128)S(1)}, u32[]{:S(2)}, u32[]{:S(2)}) async-start(f32[16,16,256]{2,1,0:T(8,128)} %bitcast), calls=%async_computation | async-start | bytes 524288 | tf_op jit(solution)/shard_map/all_to_all | solution.py:43
  200.3 11.6 %all-to-all-done = f32[16,16,256]{2,1,0:T(8,128)S(1)} async-done(((f32[16,16,256]{2,1,0:T(8,128)}), f32[16,16,256]{2,1,0:T(8,128)S(1)}, u32[]{:S(2)}, u32[]{:S(2)}) %all-to-all-start) | async-done | bytes 262176 | tf_op jit(solution)/shard_map/all_to_all | solution.py:43
  212.0 8.5 %psum.78 = f32[16]{0:T(128)S(1)} all-reduce(f32[16]{0:T(128)S(1)} %multiply_reduce_fusion.1), channel_id=1, replica_groups=mesh['wide'=16,'ctx_0'=4,'ctx_1'=4] {'ctx_0'}, use_global_device_ids=true, to_apply=%region_11.0 | all-reduce | flops 16 | bytes 128 | tf_op jit(solution)/shard_map/psum | solution.py:48
  220.5 6.5 %psum.79 = f32[16]{0:T(128)S(1)} all-reduce(f32[16]{0:T(128)S(1)} %psum.78), channel_id=1, replica_groups=mesh['wide'=16,'ctx_0'=4,'ctx_1'=4] {'ctx_1'}, use_global_device_ids=true, to_apply=%region_12.0 | all-reduce | flops 16 | bytes 128 | tf_op jit(solution)/shard_map/psum | solution.py:48
  227.2 18.4 %all_to_all.20 = f32[16,16,256]{2,1,0:T(8,128)S(1)} all-to-all(f32[16,16,256]{2,1,0:T(8,128)S(1)} %broadcast_in_dim.6), channel_id=1, replica_groups=mesh['wide'=16,'ctx_0'=4,'ctx_1'=4] {'wide'}, dimensions={0} | all-to-all | bytes 524288 | tf_op jit(solution)/shard_map/all_to_all | solution.py:59
  247.4 3.5 %all-to-all-start.2 = ((f32[16,16,256]{2,1,0:T(8,128)}), f32[16,16,256]{2,1,0:T(8,128)S(1)}, u32[]{:S(2)}, u32[]{:S(2)}) async-start(f32[16,16,256]{2,1,0:T(8,128)} %fusion.54), calls=%async_computation.2 | async-start | bytes 524288 | tf_op jit(solution)/shard_map/all_to_all | solution.py:43
  252.9 7.2 %all-to-all-done.2 = f32[16,16,256]{2,1,0:T(8,128)S(1)} async-done(((f32[16,16,256]{2,1,0:T(8,128)}), f32[16,16,256]{2,1,0:T(8,128)S(1)}, u32[]{:S(2)}, u32[]{:S(2)}) %all-to-all-start.2) | async-done | bytes 262176 | tf_op jit(solution)/shard_map/all_to_all | solution.py:43
  260.1 17.2 %all_gather.7 = f32[256,770]{1,0:T(8,128)S(1)} all-gather(f32[16,770]{1,0:T(8,128)S(1)} %pad_maximum_fusion), channel_id=1, replica_groups=mesh['wide'=16,'ctx_0'=4,'ctx_1'=4] {'ctx_0','ctx_1'}, dimensions={0}, use_global_device_ids=true | all-gather | bytes 837760 | tf_op jit(solution)/shard_map/all_gather | solution.py:70
  277.5 5.9 %collective-permute-start.2 = (f32[256,256]{0,1:T(8,128)S(1)}, f32[256,256]{0,1:T(8,128)}, u32[]{:S(2)}, u32[]{:S(2)}) collective-permute-start(f32[256,256]{0,1:T(8,128)S(1)} %copy.53), channel_id=1, source_target_pairs={{0,16},{16,0},{32,48},{48,32},{64,80},{80,64},{96,112},{112,96},{1... | collective-permute-start | bytes 786440 | tf_op jit(solution)/shard_map/ppermute | solution.py:23
  284.2 3.7 %fusion.42 = f32[256,896]{1,0:T(8,128)} fusion(f32[256,896]{1,0:T(8,128)} %get-tuple-element.6, f32[256,512]{1,0:T(8,128)S(1)} %all_gather.6, f32[256]{0:T(256)} %copy-done.23, f32[256]{0:T(256)} %param.14, f32[256,896]{1,0:T(8,128)} %get-tuple-element.7), kind=kOutput, calls=%fused_computation.43 | convolution fusion | flops 706150400 | bytes 3017728 | tf_op jit(solution)/shard_map/dot_general | solution.py:85
  292.1 4.1 %fusion.44 = f32[1024,512]{1,0:T(8,128)} fusion(f32[1024,128]{1,0:T(8,128)S(1)} %bitcast.66, f32[1,1024,128]{2,1,0:T(8,128)} %param.23), kind=kOutput, calls=%fused_computation.45 | convolution fusion | flops 805306368 | bytes 2883584 | tf_op jit(solution)/shard_map/dot_general | solution.py:91
  296.2 2.8 fusion.49
  299.1 2.1 fusion.38
  301.1 2.0 copy.42
  303.2 3.0 fusion.47
  308.1 2.2 fusion
  310.3 3.3 fusion.19
  315.7 4.2 %fusion.34 = f32[896,256]{1,0:T(8,128)} fusion(f32[256,896]{1,0:T(8,128)} %get-tuple-element.8, f32[256]{0:T(256)S(1)} %copy-done.24, f32[256,512]{1,0:T(8,128)S(1)} %all_gather.6, f32[256,896]{1,0:T(8,128)} %get-tuple-element.7), kind=kOutput, calls=%fused_computation.31 | convolution fusion | flops 706248704 | bytes 3015680 | tf_op jit(solution)/shard_map/dot_general | solution.py:85
  320.8 4.3 %all-to-all-start.3 = ((f32[16,16,256]{2,1,0:T(8,128)}), f32[16,16,256]{2,1,0:T(8,128)S(1)}, u32[]{:S(2)}, u32[]{:S(2)}) async-start(f32[16,16,256]{2,1,0:T(8,128)} %bitcast.23), calls=%async_computation.3 | async-start | bytes 524288 | tf_op jit(solution)/shard_map/all_to_all | solution.py:43
  325.1 2.0 fusion.66
  327.1 2.2 fusion.84
  329.4 4.1 %all-to-all-done.3 = f32[16,16,256]{2,1,0:T(8,128)S(1)} async-done(((f32[16,16,256]{2,1,0:T(8,128)}), f32[16,16,256]{2,1,0:T(8,128)S(1)}, u32[]{:S(2)}, u32[]{:S(2)}) %all-to-all-start.3) | async-done | bytes 262176 | tf_op jit(solution)/shard_map/all_to_all | solution.py:43
  (105 shorter events, 16.6 us)
Async XLA Ops:
  7.2 26.8 %copy-start = (f32[256,896]{1,0:T(8,128)S(1)}, f32[256,896]{1,0:T(8,128)}, u32[]{:S(2)}) copy-start(f32[256,896]{1,0:T(8,128)} %param.15) | copy-start | bytes 2752516
  7.2 26.8 %copy-start.19 = (f32[256]{0:T(256)S(1)}, f32[256]{0:T(256)}, u32[]{:S(2)}) copy-start(f32[256]{0:T(256)} %param.14) | copy-start | bytes 3076
  7.2 102.9 %all-reduce.7.cloned.1.call-start = ((), (), s32[]{:S(2)}) async-start(), calls=%async_computation.5 | async-start | bytes 5505024 | tf_op jit(solution)/shard_map/psum | solution.py:135
  30.8 5.2 %copy-start.10 = (f32[256,896]{1,0:T(8,128)S(1)}, f32[256,896]{1,0:T(8,128)}, u32[]{:S(2)}) copy-start(f32[256,896]{1,0:T(8,128)} %param.16) | copy-start | bytes 2752516
  37.9 149.0 %all-reduce.5.cloned.1.call-start = ((), (), s32[]{:S(2)}) async-start(), calls=%async_computation.4 | async-start | bytes 5505024 | tf_op jit(solution)/shard_map/psum | solution.py:134
  125.2 101.8 %copy-start.23 = (f32[256]{0:T(256)}, f32[256]{0:T(256)S(1)}, u32[]{:S(2)}) copy-start(f32[256]{0:T(256)S(1)} %add_rsqrt_fusion) | copy-start | bytes 3076
  186.9 3.4 copy-start.11
  186.9 3.4 copy-start.12
  189.2 3.0 copy-start.2
  190.3 21.6 %copy-start.15 = (f32[16,256]{1,0:T(8,128)S(1)}, f32[16,256]{1,0:T(8,128)}, u32[]{:S(2)}) copy-start(f32[16,256]{1,0:T(8,128)} %param.12) | copy-start | bytes 49156
  190.3 36.8 %copy-start.17 = (f32[16,256]{1,0:T(8,128)S(1)}, f32[16,256]{1,0:T(8,128)}, u32[]{:S(2)}) copy-start(f32[16,256]{1,0:T(8,128)} %param.13) | copy-start | bytes 49156
  190.3 56.0 %copy-start.14 = (f32[256,256]{1,0:T(8,128)S(1)}, f32[256,256]{1,0:T(8,128)}, u32[]{:S(2)}) copy-start(f32[256,256]{1,0:T(8,128)} %param.18) | copy-start | bytes 786436
  192.2 58.7 %copy-start.27 = (f32[2,16]{1,0:T(2,128)S(1)}, f32[2,16]{1,0:T(2,128)}, u32[]{:S(2)}) copy-start(f32[2,16]{1,0:T(2,128)} %param.21) | copy-start | bytes 388
  192.2 67.8 %copy-start.21 = (f32[16,256]{1,0:T(8,128)S(1)}, f32[16,256]{1,0:T(8,128)}, u32[]{:S(2)}) copy-start(f32[16,256]{1,0:T(8,128)} %param.20) | copy-start | bytes 49156
  192.2 67.8 %copy-start.22 = (f32[16,256]{1,0:T(8,128)S(1)}, f32[16,256]{1,0:T(8,128)}, u32[]{:S(2)}) copy-start(f32[16,256]{1,0:T(8,128)} %param.19) | copy-start | bytes 49156
  192.3 19.6 %all-to-all-start = ((f32[16,16,256]{2,1,0:T(8,128)}), f32[16,16,256]{2,1,0:T(8,128)S(1)}, u32[]{:S(2)}, u32[]{:S(2)}) async-start(f32[16,16,256]{2,1,0:T(8,128)} %bitcast), calls=%async_computation | async-start | bytes 524288 | tf_op jit(solution)/shard_map/all_to_all | solution.py:43
  227.2 50.2 %copy-start.16 = (f32[16,256]{1,0:T(8,128)}, f32[16,256]{1,0:T(8,128)S(1)}, u32[]{:S(2)}) copy-start(f32[16,256]{1,0:T(8,128)S(1)} %multiply_subtract_fusion) | copy-start | bytes 49156
  247.4 12.6 %all-to-all-start.2 = ((f32[16,16,256]{2,1,0:T(8,128)}), f32[16,16,256]{2,1,0:T(8,128)S(1)}, u32[]{:S(2)}, u32[]{:S(2)}) async-start(f32[16,16,256]{2,1,0:T(8,128)} %fusion.54), calls=%async_computation.2 | async-start | bytes 524288 | tf_op jit(solution)/shard_map/all_to_all | solution.py:43
  277.3 10.7 %copy-start.4 = (f32[256,770]{1,0:T(8,128)}, f32[256,770]{1,0:T(8,128)S(1)}, u32[]{:S(2)}) copy-start(f32[256,770]{1,0:T(8,128)S(1)} %all_gather.7) | copy-start | bytes 2365444
  277.5 12.5 %collective-permute-start.2 = (f32[256,256]{0,1:T(8,128)S(1)}, f32[256,256]{0,1:T(8,128)}, u32[]{:S(2)}, u32[]{:S(2)}) collective-permute-start(f32[256,256]{0,1:T(8,128)S(1)} %copy.53), channel_id=1, source_target_pairs={{0,16},{16,0},{32,48},{48,32},{64,80},{80,64},{96,112},{112,96},{1... | collective-permute-start | bytes 786440 | tf_op jit(solution)/shard_map/ppermute | solution.py:23
  283.4 5.5 %collective-permute-start.1 = (f32[2,256]{0,1:T(8,128)S(1)}, f32[2,256]{0,1:T(8,128)}, u32[]{:S(2)}, u32[]{:S(2)}) collective-permute-start(f32[2,256]{0,1:T(8,128)S(1)} %slice_bitcast_fusion), channel_id=1, source_target_pairs={{0,16},{16,0},{32,48},{48,32},{64,80},{80,64},{96,112},{112,96},{1... | collective-permute-start | bytes 6152 | tf_op jit(solution)/shard_map/ppermute | solution.py:23
  283.7 6.2 %collective-permute-start.3 = (f32[2,256]{1,0:T(2,128)S(1)}, f32[2,256]{1,0:T(2,128)S(1)}, u32[]{:S(2)}, u32[]{:S(2)}) collective-permute-start(f32[2,256]{1,0:T(2,128)S(1)} %bitcast.80), channel_id=1, source_target_pairs={{0,16},{16,0},{32,48},{48,32},{64,80},{80,64},{96,112},{112,96},{1... | collective-permute-start | bytes 6152 | tf_op jit(solution)/shard_map/ppermute | solution.py:23
  288.9 10.2 %collective-permute-start = (f32[256,256]{0,1:T(8,128)}, f32[256,256]{0,1:T(8,128)}, u32[]{:S(2)}, u32[]{:S(2)}) collective-permute-start(f32[256,256]{0,1:T(8,128)} %copy.52), channel_id=1, source_target_pairs={{0,16},{16,0},{32,48},{48,32},{64,80},{80,64},{96,112},{112,96},{1... | collective-permute-start | bytes 786440 | tf_op jit(solution)/shard_map/ppermute | solution.py:23
  291.3 4.9 %copy-start.13 = (f32[1,1024,128]{2,1,0:T(8,128)S(1)}, f32[1,1024,128]{2,1,0:T(8,128)}, u32[]{:S(2)}) copy-start(f32[1,1024,128]{2,1,0:T(8,128)} %param.23) | copy-start | bytes 1572868
  303.2 3.0 copy-start.6
  303.2 3.0 copy-start.9
  310.3 5.3 %copy-start.24 = (f32[256]{0:T(256)S(1)}, f32[256]{0:T(256)}, u32[]{:S(2)}) copy-start(f32[256]{0:T(256)} %copy-done.23) | copy-start | bytes 3076
  314.9 4.9 %collective-permute-start.4 = (f32[256,256]{0,1:T(8,128)S(1)}, f32[256,256]{0,1:T(8,128)S(1)}, u32[]{:S(2)}, u32[]{:S(2)}) collective-permute-start(f32[256,256]{0,1:T(8,128)S(1)} %slice_select_fusion), channel_id=1, source_target_pairs={{0,16},{16,0},{32,48},{48,32},{64,80},{80,64},{96,112},{112,96},{1... | collective-permute-start | bytes 786440 | tf_op jit(solution)/shard_map/ppermute | solution.py:23
  319.9 5.2 %copy-start.3 = (f32[256,896]{1,0:T(8,128)S(1)}, f32[256,896]{1,0:T(8,128)}, u32[]{:S(2)}) copy-start(f32[256,896]{1,0:T(8,128)} %copy-done.2) | copy-start | bytes 2752516
  319.9 5.2 %copy-start.20 = (f32[256]{0:T(256)S(1)}, f32[256]{0:T(256)}, u32[]{:S(2)}) copy-start(f32[256]{0:T(256)} %param.14) | copy-start | bytes 3076
  319.9 7.2 %copy-start.8 = (f32[16,16,256]{2,1,0:T(8,128)S(1)}, f32[16,16,256]{2,1,0:T(8,128)}, u32[]{:S(2)}) copy-start(f32[16,16,256]{2,1,0:T(8,128)} %copy-done.7) | copy-start | bytes 786436
  320.8 12.7 %all-to-all-start.3 = ((f32[16,16,256]{2,1,0:T(8,128)}), f32[16,16,256]{2,1,0:T(8,128)S(1)}, u32[]{:S(2)}, u32[]{:S(2)}) async-start(f32[16,16,256]{2,1,0:T(8,128)} %bitcast.23), calls=%async_computation.3 | async-start | bytes 524288 | tf_op jit(solution)/shard_map/all_to_all | solution.py:43
  (6 other events, 9.3 us)
Sparse Core Ops, SparseCore 0:
  38.0 71.9 all-reduce.6
  112.6 74.2 all-reduce.4
